TPU v7x, 32 devices: a whole 2x2x4 slice. The times are simulated.
32 devices in a mesh: tg: 8 (over y, x, core), ep: 4 (over z).
Axes of the slice: x: 2, y: 2, z: 4, core: 2. Of those that a mesh axis runs over, the one named last changes fastest.
Arguments:
- tokens: bfloat16 [16384, 384], P(('tg', 'ep')), may hold values from -6 to 6
- timesteps: int32 [64], replicated, may hold values from 0 to 999, as said below
- labels: int32 [64], replicated, may hold values from 0 to 999
- routes: int32 [16384, 2], P(('tg', 'ep')), may hold values from 0 to 15, as said below
- time_table: bfloat16 [1000, 384], replicated, may hold values from -4.1875 to 4.1875
- class_table: bfloat16 [1000, 384], replicated, may hold values from -4.1875 to 4.1875
- ada_weight: bfloat16 [384, 2304], replicated, may hold values from -0.3125 to 0.3125
- ada_bias: float32 [2304], replicated, may hold values from -3 to 3
- gain_attn: float32 [384], replicated, may hold values from 0.5 to 1.5
- gain_ffn: float32 [384], replicated, may hold values from 0.5 to 1.5
- qkv_weight: bfloat16 [384, 1152], replicated, may hold values from -0.3125 to 0.3125
- proj_weight: bfloat16 [384, 384], replicated, may hold values from -1.25 to 1.25
- router_weight: bfloat16 [384, 16], replicated, may hold values from -0.625 to 0.625
- shared_in: bfloat16 [384, 3072], replicated, may hold values from -0.3125 to 0.3125
- shared_out: bfloat16 [3072, 384], replicated, may hold values from -0.15625 to 0.15625
- expert_in: bfloat16 [16, 384, 1536], P('ep', None, 'tg'), may hold values from -0.3125 to 0.3125
- expert_out: bfloat16 [16, 1536, 384], P('ep', 'tg'), may hold values from -0.15625 to 0.15625
- grad_out: bfloat16 [16384, 384], P(('tg', 'ep')), may hold values from -6 to 6
Outputs:
- out: bfloat16 [16384, 384], P(('tg', 'ep'))
- grad_tokens: float32 [16384, 384], P(('tg', 'ep'))
- grad_time_table: float32 [1000, 384], replicated
- grad_class_table: float32 [1000, 384], replicated
- grad_ada_weight: float32 [384, 2304], replicated
- grad_ada_bias: float32 [2304], replicated
- grad_gain_attn: float32 [384], replicated
- grad_gain_ffn: float32 [384], replicated
- grad_qkv_weight: float32 [384, 1152], replicated
- grad_proj_weight: float32 [384, 384], replicated
- grad_router: float32 [384, 16], replicated
- grad_shared_in: float32 [384, 3072], replicated
- grad_shared_out: float32 [3072, 384], replicated
- grad_expert_in: float32 [16, 384, 1536], P('ep', None, 'tg')
- grad_expert_out: float32 [16, 1536, 384], P('ep', 'tg')
Inputs may be any that keep to these rules, and one draw needn't show every extreme that they name: With G = 8 groups, the images g * 8 to (g + 1) * 8 - 1 have timesteps t with g * 1000 <= G * t < (g + 1) * 1000; the first image of each group has the smallest such t and the last image the largest. `routes`: each row names two different experts. In the rows of one device no expert is named by more than 256 rows. For each group of 2048 rows (one index of tg) one expert is named by exactly 256 rows on every device of the group.
All inputs are finite; a program needn't handle non-finite values.
Results may differ from a plain program's by a relative error of at most 0.015.
The roundings to bfloat16 on the way count: a program that leaves them out, or rounds other values in their place, can miss the bound.
Values may be sent and summed in bfloat16 or wider, within the bound.
No kernel may reach another device: no remote copies, remote signals or barrier semaphores. Data moves between devices by JAX's collectives and lax.ppermute only.
A program may use at most 192 MiB of HBM per device.

v0:
```python
import jax
import jax.numpy as jnp
from jax import lax
from jax.sharding import PartitionSpec as P

HEAD_DIM = 64
PATCHES = 256


def normalize(values):
    centred = values - jnp.mean(values, axis=-1, keepdims=True)
    inverse = lax.rsqrt(jnp.mean(centred * centred, axis=-1, keepdims=True) + 1e-06)
    return (centred * inverse, inverse)


def norm_back(grad_normed, normed, inverse):
    mean_grad = jnp.mean(grad_normed, axis=-1, keepdims=True)
    mean_cross = jnp.mean(grad_normed * normed, axis=-1, keepdims=True)
    return inverse * (grad_normed - mean_grad - normed * mean_cross)


def gelu_tanh(values):
    return jax.nn.gelu(values, approximate=True)


def gelu_back(values, grad_values):
    return jax.vjp(gelu_tanh, values)[1](grad_values)[0]


def route_gates(logits, first_hot, second_hot):
    peak_value = jnp.max(logits, axis=-1, keepdims=True)
    shifted = jnp.exp(logits - peak_value)
    probability = shifted / jnp.sum(shifted, axis=-1, keepdims=True)
    first_prob = jnp.sum(probability * first_hot, axis=-1)
    second_prob = jnp.sum(probability * second_hot, axis=-1)
    denominator = first_prob + second_prob
    return jnp.stack([first_prob / denominator, second_prob / denominator], axis=-1)


def split_heads(qkv_block):
    block_count, patches, triple = qkv_block.shape
    features = triple // 3
    head_shape = (block_count, patches, features // HEAD_DIM, HEAD_DIM)
    return (
        qkv_block[..., :features].reshape(head_shape),
        qkv_block[..., features : 2 * features].reshape(head_shape),
        qkv_block[..., 2 * features :].reshape(head_shape),
    )


def attend_forward(qkv_block):
    queries, key_rows, value_rows = split_heads(qkv_block)
    score_scale = HEAD_DIM ** (-0.5)
    scores = (
        jnp.einsum("bqhd,bkhd->bhqk", queries, key_rows, preferred_element_type=jnp.float32)
        * score_scale
    )
    peak_value = jnp.max(scores, axis=-1, keepdims=True)
    shifted = jnp.exp(scores - peak_value)
    denominator = jnp.sum(shifted, axis=-1, keepdims=True)
    probability = (shifted / denominator).astype(jnp.bfloat16)
    mixed_rows = jnp.einsum(
        "bhqk,bkhd->bqhd", probability, value_rows, preferred_element_type=jnp.float32
    )
    mixed_rows = mixed_rows.reshape(qkv_block.shape[0], qkv_block.shape[1], -1).astype(jnp.bfloat16)
    return (mixed_rows, (peak_value + jnp.log(denominator))[..., 0])


def attend_backward(packed):
    qkv_block, grad_mixed, log_total = packed
    queries, key_rows, value_rows = split_heads(qkv_block)
    score_scale = HEAD_DIM ** (-0.5)
    scores = (
        jnp.einsum("bqhd,bkhd->bhqk", queries, key_rows, preferred_element_type=jnp.float32)
        * score_scale
    )
    probability = jnp.exp(scores - log_total[..., None])
    grad_heads = grad_mixed.reshape(queries.shape)
    grad_values = jnp.einsum(
        "bhqk,bqhd->bkhd",
        probability.astype(jnp.bfloat16),
        grad_heads,
        preferred_element_type=jnp.float32,
    )
    grad_probs = jnp.einsum(
        "bqhd,bkhd->bhqk", grad_heads, value_rows, preferred_element_type=jnp.float32
    )
    grad_scores = (
        probability * (grad_probs - jnp.sum(grad_probs * probability, axis=-1, keepdims=True))
    ).astype(jnp.bfloat16)
    grad_queries = (
        jnp.einsum("bhqk,bkhd->bqhd", grad_scores, key_rows, preferred_element_type=jnp.float32)
        * score_scale
    )
    grad_keys = (
        jnp.einsum("bhqk,bqhd->bkhd", grad_scores, queries, preferred_element_type=jnp.float32)
        * score_scale
    )
    merged = jnp.concatenate([grad_queries, grad_keys, grad_values], axis=2)
    return merged.reshape(qkv_block.shape[0], qkv_block.shape[1], -1).astype(jnp.bfloat16)


def shards(
    tokens,
    timesteps,
    labels,
    routes,
    time_table,
    class_table,
    ada_weight,
    ada_bias,
    gain_attn,
    gain_ffn,
    qkv_weight,
    proj_weight,
    router_weight,
    shared_in,
    shared_out,
    expert_in,
    expert_out,
    grad_out,
):
    count_tokens, features = tokens.shape
    images = count_tokens // PATCHES
    pair_count = images // 2
    experts = router_weight.shape[1]
    capacity = count_tokens // 2
    slot_count = experts * capacity
    ep_size = lax.axis_size("ep")
    device = lax.axis_index("tg") * ep_size + lax.axis_index("ep")
    steps_here = lax.dynamic_slice_in_dim(timesteps, device * images, images)
    labels_here = lax.dynamic_slice_in_dim(labels, device * images, images)
    step_ids = jnp.arange(time_table.shape[0], dtype=jnp.int32)
    class_ids = jnp.arange(class_table.shape[0], dtype=jnp.int32)
    time_hot = (steps_here[:, None] == step_ids[None, :]).astype(jnp.bfloat16)
    class_hot = (labels_here[:, None] == class_ids[None, :]).astype(jnp.bfloat16)
    condition = jnp.dot(time_hot, time_table, preferred_element_type=jnp.float32) + jnp.dot(
        class_hot, class_table, preferred_element_type=jnp.float32
    )
    silu_low = jax.nn.silu(condition).astype(jnp.bfloat16)
    modulation = (
        jnp.dot(silu_low, ada_weight, preferred_element_type=jnp.float32) + ada_bias
    ).reshape(images, 6, 1, features)
    residual = tokens.astype(jnp.float32).reshape(images, PATCHES, features)
    normed_attn, inverse_attn = normalize(residual)
    factor_attn = 1.0 + modulation[:, 1]
    attn_in = (
        (normed_attn * gain_attn * factor_attn + modulation[:, 0])
        .astype(jnp.bfloat16)
        .reshape(-1, features)
    )
    qkv_rows = jnp.dot(attn_in, qkv_weight, preferred_element_type=jnp.float32).astype(jnp.bfloat16)
    qkv_blocks = qkv_rows.reshape(pair_count, 2, PATCHES, 3 * features)
    mixed_rows, log_total = lax.map(attend_forward, qkv_blocks)
    mixed_rows = mixed_rows.reshape(-1, features)
    attn_out = jnp.dot(mixed_rows, proj_weight, preferred_element_type=jnp.float32).reshape(
        images, PATCHES, features
    )
    middle = residual + modulation[:, 2] * attn_out
    normed_ffn, inverse_ffn = normalize(middle)
    factor_ffn = 1.0 + modulation[:, 4]
    ffn_in = (
        (normed_ffn * gain_ffn * factor_ffn + modulation[:, 3])
        .astype(jnp.bfloat16)
        .reshape(-1, features)
    )
    expert_ids = jnp.arange(experts, dtype=jnp.int32)
    first_int = (routes[:, 0:1] == expert_ids[None, :]).astype(jnp.int32)
    second_int = (routes[:, 1:2] == expert_ids[None, :]).astype(jnp.int32)
    first_hot = first_int.astype(jnp.float32)
    second_hot = second_int.astype(jnp.float32)
    logits = jnp.dot(ffn_in, router_weight, preferred_element_type=jnp.float32)
    gate_values, gate_pullback = jax.vjp(
        lambda values: route_gates(values, first_hot, second_hot), logits
    )
    both_int = first_int + second_int
    before = jnp.cumsum(both_int, axis=0) - both_int
    first_slot = routes[:, 0] * capacity + jnp.sum(before * first_int, axis=1)
    second_slot = routes[:, 1] * capacity + jnp.sum(before * second_int, axis=1)
    token_ids = jnp.arange(count_tokens, dtype=jnp.int32)
    source_rows = jnp.full((slot_count,), 2 * count_tokens, jnp.int32)
    source_rows = source_rows.at[jnp.concatenate([first_slot, second_slot])].set(
        jnp.concatenate([token_ids, token_ids + count_tokens])
    )
    token_rows = jnp.where(source_rows < 2 * count_tokens, source_rows % count_tokens, count_tokens)
    padded_in = jnp.concatenate([ffn_in, jnp.zeros((1, features), jnp.bfloat16)], axis=0)
    dispatch_rows = padded_in[token_rows].reshape(experts, capacity, features)
    received = lax.all_to_all(dispatch_rows, "ep", split_axis=0, concat_axis=1, tiled=True)
    full_in, full_out = (
        lax.all_gather(expert_in, "tg", axis=2, tiled=True),
        lax.all_gather(expert_out, "tg", axis=1, tiled=True),
    )
    hidden = jnp.einsum("erd,edf->erf", received, full_in, preferred_element_type=jnp.float32)
    active = gelu_tanh(hidden).astype(jnp.bfloat16)
    produced = jnp.einsum(
        "erf,efd->erd", active, full_out, preferred_element_type=jnp.float32
    ).astype(jnp.bfloat16)
    returned = lax.all_to_all(produced, "ep", split_axis=1, concat_axis=0, tiled=True).reshape(
        slot_count, features
    )
    first_out = returned[first_slot].astype(jnp.float32)
    second_out = returned[second_slot].astype(jnp.float32)
    routed = gate_values[:, 0:1] * first_out + gate_values[:, 1:2] * second_out
    shared_hidden = jnp.dot(ffn_in, shared_in, preferred_element_type=jnp.float32)
    shared_active = gelu_tanh(shared_hidden).astype(jnp.bfloat16)
    shared_term = jnp.dot(shared_active, shared_out, preferred_element_type=jnp.float32)
    ffn_out = (routed + shared_term).reshape(images, PATCHES, features)
    output = (middle + modulation[:, 5] * ffn_out).reshape(-1, features).astype(jnp.bfloat16)
    upstream = grad_out.astype(jnp.float32).reshape(images, PATCHES, features)
    grad_gate_ffn = jnp.sum(upstream * ffn_out, axis=1)
    grad_ffn = (modulation[:, 5] * upstream).reshape(-1, features)
    grad_shared_low = grad_ffn.astype(jnp.bfloat16)
    grad_shared_out = jnp.einsum(
        "rf,rd->fd", shared_active, grad_shared_low, preferred_element_type=jnp.float32
    )
    grad_shared_active = jnp.einsum(
        "rd,fd->rf", grad_shared_low, shared_out, preferred_element_type=jnp.float32
    )
    grad_shared_hidden = gelu_back(shared_hidden, grad_shared_active).astype(jnp.bfloat16)
    grad_shared_in = jnp.einsum(
        "rd,rf->df", ffn_in, grad_shared_hidden, preferred_element_type=jnp.float32
    )
    grad_ffn_in = jnp.einsum(
        "rf,df->rd", grad_shared_hidden, shared_in, preferred_element_type=jnp.float32
    )
    grad_first = (gate_values[:, 0:1] * grad_ffn).astype(jnp.bfloat16)
    grad_second = (gate_values[:, 1:2] * grad_ffn).astype(jnp.bfloat16)
    grad_gates = jnp.stack(
        [jnp.sum(grad_ffn * first_out, axis=1), jnp.sum(grad_ffn * second_out, axis=1)], axis=1
    )
    padded_grad = jnp.concatenate(
        [grad_first, grad_second, jnp.zeros((1, features), jnp.bfloat16)], axis=0
    )
    grad_rows = padded_grad[source_rows].reshape(experts, capacity, features)
    grad_received = lax.all_to_all(grad_rows, "ep", split_axis=0, concat_axis=1, tiled=True)
    back_in, back_out = (
        lax.all_gather(expert_in, "tg", axis=2, tiled=True),
        lax.all_gather(expert_out, "tg", axis=1, tiled=True),
    )
    grad_active = jnp.einsum(
        "erd,efd->erf", grad_received, back_out, preferred_element_type=jnp.float32
    )
    grad_expert_out = jnp.einsum(
        "erf,erd->efd", active, grad_received, preferred_element_type=jnp.float32
    )
    grad_hidden = gelu_back(hidden, grad_active).astype(jnp.bfloat16)
    grad_expert_in = jnp.einsum(
        "erd,erf->edf", received, grad_hidden, preferred_element_type=jnp.float32
    )
    grad_sent = jnp.einsum(
        "erf,edf->erd", grad_hidden, back_in, preferred_element_type=jnp.float32
    ).astype(jnp.bfloat16)
    grad_back = lax.all_to_all(grad_sent, "ep", split_axis=1, concat_axis=0, tiled=True).reshape(
        slot_count, features
    )
    grad_ffn_in = (
        grad_ffn_in
        + grad_back[first_slot].astype(jnp.float32)
        + grad_back[second_slot].astype(jnp.float32)
    )
    shard_in, shard_out = (
        lax.psum_scatter(
            grad_expert_in.astype(jnp.bfloat16), "tg", scatter_dimension=2, tiled=True
        ).astype(jnp.float32),
        lax.psum_scatter(
            grad_expert_out.astype(jnp.bfloat16), "tg", scatter_dimension=1, tiled=True
        ).astype(jnp.float32),
    )
    grad_logits = gate_pullback(grad_gates)[0]
    grad_router = jnp.einsum(
        "rd,re->de", ffn_in.astype(jnp.float32), grad_logits, precision=lax.Precision.HIGHEST
    )
    grad_ffn_in = grad_ffn_in + jnp.einsum(
        "re,de->rd", grad_logits, router_weight.astype(jnp.float32), precision=lax.Precision.HIGHEST
    )
    grad_ffn_cube = grad_ffn_in.reshape(images, PATCHES, features)
    grad_shift_ffn = jnp.sum(grad_ffn_cube, axis=1)
    grad_scale_ffn = jnp.sum(grad_ffn_cube * normed_ffn, axis=1) * gain_ffn
    grad_gain_ffn = jnp.sum(grad_ffn_cube * normed_ffn * factor_ffn, axis=(0, 1))
    grad_middle = upstream + norm_back(
        grad_ffn_cube * gain_ffn * factor_ffn, normed_ffn, inverse_ffn
    )
    grad_gate_attn = jnp.sum(grad_middle * attn_out, axis=1)
    grad_attn_low = (modulation[:, 2] * grad_middle).reshape(-1, features).astype(jnp.bfloat16)
    grad_proj = jnp.einsum(
        "rd,re->de", mixed_rows, grad_attn_low, preferred_element_type=jnp.float32
    )
    grad_mixed = jnp.einsum(
        "re,de->rd", grad_attn_low, proj_weight, preferred_element_type=jnp.float32
    ).astype(jnp.bfloat16)
    grad_qkv = lax.map(
        attend_backward,
        (qkv_blocks, grad_mixed.reshape(pair_count, 2, PATCHES, features), log_total),
    ).reshape(-1, 3 * features)
    grad_qkv_weight = jnp.einsum("rd,re->de", attn_in, grad_qkv, preferred_element_type=jnp.float32)
    grad_attn_in = jnp.einsum(
        "re,de->rd", grad_qkv, qkv_weight, preferred_element_type=jnp.float32
    ).reshape(images, PATCHES, features)
    grad_shift_attn = jnp.sum(grad_attn_in, axis=1)
    grad_scale_attn = jnp.sum(grad_attn_in * normed_attn, axis=1) * gain_attn
    grad_gain_attn = jnp.sum(grad_attn_in * normed_attn * factor_attn, axis=(0, 1))
    grad_tokens = grad_middle + norm_back(
        grad_attn_in * gain_attn * factor_attn, normed_attn, inverse_attn
    )
    grad_modulation = jnp.stack(
        [
            grad_shift_attn,
            grad_scale_attn,
            grad_gate_attn,
            grad_shift_ffn,
            grad_scale_ffn,
            grad_gate_ffn,
        ],
        axis=1,
    ).reshape(images, 6 * features)
    grad_ada_bias = jnp.sum(grad_modulation, axis=0)
    grad_ada_weight = jnp.einsum(
        "id,ie->de", silu_low.astype(jnp.float32), grad_modulation, precision=lax.Precision.HIGHEST
    )
    grad_silu = jnp.einsum(
        "ie,de->id",
        grad_modulation,
        ada_weight.astype(jnp.float32),
        precision=lax.Precision.HIGHEST,
    )
    grad_condition = jax.vjp(jax.nn.silu, condition)[1](grad_silu)[0]
    time_term = jnp.einsum(
        "is,id->sd", time_hot.astype(jnp.float32), grad_condition, precision=lax.Precision.HIGHEST
    )
    class_term = jnp.einsum(
        "ic,id->cd", class_hot.astype(jnp.float32), grad_condition, precision=lax.Precision.HIGHEST
    )
    totals = lax.psum(
        (
            grad_qkv_weight,
            grad_proj,
            grad_ada_weight,
            grad_ada_bias,
            grad_gain_attn,
            grad_gain_ffn,
            grad_router,
            grad_shared_in,
            grad_shared_out,
            time_term,
            class_term,
        ),
        ("tg", "ep"),
    )
    grad_time_table = totals[9]
    grad_class_table = totals[10]
    return (
        output,
        grad_tokens.reshape(-1, features),
        grad_time_table,
        grad_class_table,
        totals[2],
        totals[3],
        totals[4],
        totals[5],
        totals[0],
        totals[1],
        totals[6],
        totals[7],
        totals[8],
        shard_in,
        shard_out,
    )


def solution(mesh):
    in_specs = (
        P(("tg", "ep"), None),
        P(),
        P(),
        P(("tg", "ep"), None),
        P(),
        P(),
        P(),
        P(),
        P(),
        P(),
        P(),
        P(),
        P(),
        P(),
        P(),
        P("ep", None, "tg"),
        P("ep", "tg", None),
        P(("tg", "ep"), None),
    )
    out_specs = (
        P(("tg", "ep"), None),
        P(("tg", "ep"), None),
        P(),
        P(),
        P(),
        P(),
        P(),
        P(),
        P(),
        P(),
        P(),
        P(),
        P(),
        P("ep", None, "tg"),
        P("ep", "tg", None),
    )
    return jax.shard_map(shards, mesh=mesh, in_specs=in_specs, out_specs=out_specs, check_vma=False)
```

profile of v0, /device:TPU:0, one launch (start us, length us, event | category | flops | bytes accessed | tf_op | source)
XLA Modules:
  0.0 867.3 jit_solution(16981801930494201926)
XLA Ops:
  10.2 1.4 fusion.74
  11.6 1.4 convolution_add_fusion.4
  13.6 1.8 convolution_add_fusion
  17.4 2.1 convolution_convert_fusion.2
  20.7 1.3 copy.99
  22.0 2.1 copy.97
  26.5 1.3 multiply_add_fusion.2
  34.5 4.3 scatter_custom_fusion
  39.4 17.1 %gather_fusion = bf16[4096,384]{1,0:T(8,128)(2,1)} fusion(bf16[513,384]{1,0:T(8,128)(2,1)S(1)} %concatenate.35, s32[4096]{0:T(1024)S(1)} %get-tuple-element.94), kind=kCustom, calls=%fused_computation | custom fusion | bytes 6307840 | tf_op jit(solution)/shard_map/gather | solution.py:187
  56.5 77.5 %all_to_all.66 = bf16[16,256,384]{2,1,0:T(8,128)(2,1)S(1)} all-to-all(bf16[16,256,384]{2,1,0:T(8,128)(2,1)} %bitcast.220), channel_id=1, replica_groups=mesh['tg'=8,'ep'=4] {'ep'}, dimensions={0} | all-to-all | bytes 6291456 | tf_op jit(solution)/shard_map/all_to_all | solution.py:188
  134.1 2.1 copy.103
  136.2 19.7 %multiply_convert_fusion = (bf16[4,1024,1536]{2,1,0:T(8,128)(2,1)}, f32[4,1024,1536]{2,1,0:T(8,128)}) fusion(bf16[4,1024,384]{2,1,0:T(8,128)(2,1)} %bitcast.240, bf16[4,384,1536]{1,2,0:T(8,128)(2,1)} %all-gather.3.cloned.1.call-done), kind=kOutput, calls=%fused_computation.16 | convolution fusion | flops 4888461312 | bytes 45613056 | tf_op jit(solution)/shard_map/erd,edf->erf/dot_general | solution.py:193
  155.9 11.0 %convolution_convert_fusion.4 = bf16[4,1024,384]{2,1,0:T(8,128)(2,1)S(1)} fusion(bf16[4,1024,1536]{2,1,0:T(8,128)(2,1)} %get-tuple-element.107, bf16[4,1536,384]{2,1,0:T(8,128)(2,1)} %all-gather.5.cloned.1.call-done), kind=kOutput, calls=%fused_computation.41 | convolution fusion | flops 4833411072 | bytes 20447232 | tf_op jit(solution)/shard_map/erf,efd->erd/dot_general | solution.py:195
  166.9 4.1 copy.104
  171.0 4.9 all-to-all-start.1
  180.4 65.5 %all-to-all-done.1 = bf16[4,1024,384]{2,0,1:T(4,128)(2,1)} async-done(((bf16[4,1024,384]{2,0,1:T(4,128)(2,1)}), bf16[4,1024,384]{2,0,1:T(4,128)(2,1)}, u32[]{:S(2)}, u32[]{:S(2)}) %all-to-all-start.1) | async-done | bytes 3145760 | tf_op jit(solution)/shard_map/all_to_all | solution.py:198
  245.9 4.1 copy.105
  250.0 4.2 gather_fusion.1
  254.2 4.9 gather_fusion.2
  259.1 2.7 fusion.32
  262.7 18.4 %gather_fusion.3 = bf16[4096,384]{1,0:T(8,128)(2,1)} fusion(bf16[1025,384]{1,0:T(8,128)(2,1)S(1)} %maximum_maximum_fusion, s32[4096]{0:T(1024)} %get-tuple-element.93), kind=kCustom, calls=%fused_computation.3 | custom fusion | bytes 6307840 | tf_op jit(solution)/shard_map/gather | solution.py:234
  281.1 4.8 all-to-all-start.2
  288.5 6.1 fusion.95
  295.3 60.8 %all-to-all-done.2 = bf16[16,256,384]{2,1,0:T(8,128)(2,1)} async-done(((bf16[16,256,384]{2,1,0:T(8,128)(2,1)}), bf16[16,256,384]{2,1,0:T(8,128)(2,1)}, u32[]{:S(2)}, u32[]{:S(2)}) %all-to-all-start.2) | async-done | bytes 3145760 | tf_op jit(solution)/shard_map/all_to_all | solution.py:235
  356.2 2.2 copy.106
  358.4 1.7 copy-done.17
  360.0 11.4 %convolution_convert_fusion = bf16[4,1536,384]{2,1,0:T(8,128)(2,1)} fusion(bf16[4,1024,1536]{2,1,0:T(8,128)(2,1)} %get-tuple-element.107, bf16[4,1024,384]{2,1,0:T(8,128)(2,1)S(1)} %bitcast.242), kind=kOutput, calls=%fused_computation.27 | convolution fusion | flops 4834197504 | bytes 20447232 | tf_op jit(solution)/shard_map/erf,erd->efd/dot_general | solution.py:243
  371.5 27.1 %fusion.6 = bf16[4,1024,1536]{2,1,0:T(8,128)(2,1)} fusion(f32[4,1024,1536]{2,1,0:T(8,128)} %get-tuple-element.108, bf16[4,1024,384]{2,1,0:T(8,128)(2,1)} %bitcast.243, bf16[4,1536,384]{2,1,0:T(8,128)(2,1)} %all-gather.5.cloned.1.call-done), kind=kOutput, calls=%fused_computation.15 | convolution fusion | flops 4957667328 | bytes 45613056 | tf_op jit(solution)/shard_map/erd,efd->erf/dot_general | solution.py:240
  398.5 11.1 %convolution_convert_fusion.3 = bf16[4,1024,384]{2,1,0:T(8,128)(2,1)S(1)} fusion(bf16[4,1024,1536]{2,1,0:T(8,128)(2,1)} %fusion.6, bf16[4,384,1536]{1,2,0:T(8,128)(2,1)} %all-gather.3.cloned.1.call-done), kind=kOutput, calls=%fused_computation.40 | convolution fusion | flops 4833411072 | bytes 20447232 | tf_op jit(solution)/shard_map/erf,edf->erd/dot_general | solution.py:250
  409.7 4.1 copy.107
  413.8 4.8 all-to-all-start.3
  419.2 7.3 fusion.13
  426.5 1.7 copy-done.18
  428.2 3.6 fusion.98
  431.9 7.7 fusion.88
  439.6 4.0 multiply_reduce_fusion.4
  443.7 11.2 %convolution_convert_fusion.1 = bf16[4,384,1536]{1,2,0:T(8,128)(2,1)} fusion(bf16[4,1024,384]{2,1,0:T(8,128)(2,1)S(1)} %bitcast.241, bf16[4,1024,1536]{2,1,0:T(8,128)(2,1)} %fusion.6), kind=kOutput, calls=%fused_computation.28 | convolution fusion | flops 4834197504 | bytes 20447232 | tf_op jit(solution)/shard_map/erd,erf->edf/dot_general | solution.py:247
  454.9 33.8 %all-to-all-done.3 = bf16[4,1024,384]{2,0,1:T(4,128)(2,1)} async-done(((bf16[4,1024,384]{2,0,1:T(4,128)(2,1)}), bf16[4,1024,384]{2,0,1:T(4,128)(2,1)}, u32[]{:S(2)}, u32[]{:S(2)}) %all-to-all-start.3) | async-done | bytes 3145760 | tf_op jit(solution)/shard_map/all_to_all | solution.py:253
  488.8 4.1 copy.108
  492.9 4.7 gather_fusion.4
  497.7 4.9 gather_fusion.5
  502.7 4.7 fusion.26
  507.4 1.5 fusion.33
  509.5 1.3 div.113
  510.7 2.5 multiply_reduce_fusion.2
  513.2 3.6 multiply_reduce_fusion.5
  520.2 3.1 multiply_reduce_fusion
  526.3 1.9 convolution_bitcast_fusion
  528.3 2.6 multiply_reduce_fusion.3
  532.3 1.5 fusion.96
  533.8 2.2 fusion.72
  536.0 2.2 fusion.73
  538.2 3.6 fusion.85
  542.9 41.2 %all-reduce.1 = (f32[2304]{0:T(1024)}, f32[384]{0:T(512)}, f32[384]{0:T(512)}, f32[384,16]{0,1:T(8,128)}) all-reduce(f32[2304]{0:T(1024)S(1)} %reduce_sum.312, f32[384]{0:T(512)S(1)} %copy-done.99, f32[384]{0:T(512)S(1)} %copy-done.89, f32[384,16]{0,1:T(8,128)S(1)} %fusion.59), channel_id=1, replica_groups=mesh['tg'=8,'ep'=4] {'tg','ep'}, use_global_device_ids=true, to_apply=%region_35.36 | all-reduce | flops 9216 | bytes 73728 | tf_op jit(solution)/shard_map/psum | solution.py:333
  584.1 2.6 multiply_add_fusion
  586.8 2.2 convert_element_type.208
  589.0 2.2 convert_element_type.206
  591.1 253.0 %all-reduce.5.cloned.1.call-done = (f32[1000,384]{1,0:T(8,128)}, f32[1000,384]{1,0:T(8,128)}, f32[384,2304]{1,0:T(8,128)}, f32[384,1152]{1,0:T(8,128)}, f32[384,...) async-done(((f32[1000,384]{1,0:T(8,128)}, f32[1000,384]{1,0:T(8,128)}, f32[384,2304]{1,0:T(8,128)}, f32[384,1152]{1,0:T(8,128)}, f32[384,384]{1,0:T(8,128)}, ...) | async-done | bytes 18407440 | tf_op jit(solution)/shard_map/psum | solution.py:333
  844.2 2.8 copy.168
  847.0 2.8 copy.169
  849.7 1.8 copy.170
  852.5 1.2 copy.171
  854.8 2.4 copy.173
  858.3 2.2 copy.174
  (317 shorter events, 37.8 us)
Async XLA Ops:
  7.2 412.0 %copy-start = (bf16[3072,384]{1,0:T(8,128)(2,1)S(1)}, bf16[3072,384]{1,0:T(8,128)(2,1)}, u32[]{:S(2)}) copy-start(bf16[3072,384]{1,0:T(8,128)(2,1)} %param.32) | copy-start | bytes 7077892
  7.2 8.8 %copy-start.5 = (bf16[512,384]{1,0:T(8,128)(2,1)S(1)}, bf16[512,384]{1,0:T(8,128)(2,1)}, u32[]{:S(2)}) copy-start(bf16[512,384]{1,0:T(8,128)(2,1)} %param.18) | copy-start | bytes 1179652
  7.2 9.9 %copy-start.74 = (f32[384]{0:T(512)S(1)}, f32[384]{0:T(512)}, u32[]{:S(2)}) copy-start(f32[384]{0:T(512)} %param.26) | copy-start | bytes 4612
  7.2 128.9 %all-gather.3.cloned.1.call-start = ((), (), s32[]{:S(2)}) async-start(), calls=%async_computation.6 | async-start | bytes 5308416 | tf_op jit(solution)/shard_map/all_gather | solution.py:190
  8.0 147.9 %all-gather.5.cloned.1.call-start = ((), (), s32[]{:S(2)}) async-start(), calls=%async_computation.7 | async-start | bytes 5308416 | tf_op jit(solution)/shard_map/all_gather | solution.py:191
  16.5 9.9 %copy-start.70 = (f32[2,384]{1,0:T(2,128)}, f32[2,384]{1,0:T(2,128)S(1)}, u32[]{:S(2)}) copy-start(f32[2,384]{1,0:T(2,128)S(1)} %get-tuple-element.123) | copy-start | bytes 9220
  26.4 5.4 copy-start.56
  27.8 4.9 copy-start.3
  28.0 28.5 %copy-start.55 = (f32[2,256]{1,0:T(2,128)}, f32[2,256]{1,0:T(2,128)S(1)}, u32[]{:S(2)}) copy-start(f32[2,256]{1,0:T(2,128)S(1)} %broadcast_multiply_fusion.3) | copy-start | bytes 6148
  29.6 147.8 %copy-start.49 = (s32[512,1]{0,1:T(1,128)}, s32[512,1]{0,1:T(1,128)S(1)}, u32[]{:S(2)}) copy-start(s32[512,1]{0,1:T(1,128)S(1)} %get-tuple-element.101) | copy-start | bytes 6148
  29.6 147.8 %copy-start.51 = (s32[512,1]{0,1:T(1,128)}, s32[512,1]{0,1:T(1,128)S(1)}, u32[]{:S(2)}) copy-start(s32[512,1]{0,1:T(1,128)S(1)} %get-tuple-element.102) | copy-start | bytes 6148
  171.0 6.1 copy-start.61
  171.0 74.9 %all-to-all-start.1 = ((bf16[4,1024,384]{2,0,1:T(4,128)(2,1)}), bf16[4,1024,384]{2,0,1:T(4,128)(2,1)}, u32[]{:S(2)}, u32[]{:S(2)}) async-start(bf16[4,1024,384]{2,0,1:T(4,128)(2,1)} %copy.104), calls=%async_computation.1 | async-start | bytes 6291456 | tf_op jit(solution)/shard_map/all_to_all | solution.py:198
  177.2 77.0 %copy-start.82 = (s32[1024]{0:T(1024)}, s32[1024]{0:T(1024)S(1)}, u32[]{:S(2)}) copy-start(s32[1024]{0:T(1024)S(1)} %get-tuple-element.124) | copy-start | bytes 12292
  178.0 110.3 %copy-start.65 = (f32[512]{0:T(512)}, f32[512]{0:T(512)S(1)}, u32[]{:S(2)}) copy-start(f32[512]{0:T(512)S(1)} %fusion.61) | copy-start | bytes 6148
  250.0 9.1 %copy-start.20 = (bf16[512,384]{1,0:T(8,128)(2,1)S(1)}, bf16[512,384]{1,0:T(8,128)(2,1)}, u32[]{:S(2)}) copy-start(bf16[512,384]{1,0:T(8,128)(2,1)} %param.35) | copy-start | bytes 1179652
  250.0 9.1 %copy-start.69 = (f32[2,384]{1,0:T(2,128)S(1)}, f32[2,384]{1,0:T(2,128)}, u32[]{:S(2)}) copy-start(f32[2,384]{1,0:T(2,128)} %get-tuple-element.120) | copy-start | bytes 9220
  254.2 7.6 copy-start.22
  254.2 4.9 copy-start.92
  281.1 4.9 copy-start.77
  281.1 5.5 copy-start.64
  281.1 6.1 copy-start.28
  281.1 7.3 copy-start.42
  281.1 7.3 copy-start.54
  281.1 75.1 %all-to-all-start.2 = ((bf16[16,256,384]{2,1,0:T(8,128)(2,1)}), bf16[16,256,384]{2,1,0:T(8,128)(2,1)}, u32[]{:S(2)}, u32[]{:S(2)}) async-start(bf16[16,256,384]{2,1,0:T(8,128)(2,1)} %bitcast.219), calls=%async_computation.2 | async-start | bytes 6291456 | tf_op jit(solution)/shard_map/all_to_all | solution.py:235
  285.9 300.9 %reduce-scatter.5.cloned.1.call-start = ((), (), s32[]{:S(2)}) async-start(), calls=%async_computation.9 | async-start | bytes 5308416 | tf_op jit(solution)/shard_map/reduce_scatter | solution.py:265
  288.4 6.2 copy-start.79
  288.4 6.2 copy-start.81
  288.4 6.2 copy-start.95
  288.4 6.2 copy-start.96
  288.4 6.2 copy-start.33
  288.4 6.2 copy-start.50
  288.5 6.2 copy-start.52
  288.5 6.2 copy-start.60
  288.5 6.2 copy-start.66
  413.8 4.8 copy-start.97
  413.8 5.4 copy-start.35
  413.8 75.0 %all-to-all-start.3 = ((bf16[4,1024,384]{2,0,1:T(4,128)(2,1)}), bf16[4,1024,384]{2,0,1:T(4,128)(2,1)}, u32[]{:S(2)}, u32[]{:S(2)}) async-start(bf16[4,1024,384]{2,0,1:T(4,128)(2,1)} %copy.107), calls=%async_computation.3 | async-start | bytes 6291456 | tf_op jit(solution)/shard_map/all_to_all | solution.py:253
  418.6 170.4 %reduce-scatter.3.cloned.1.call-start = ((), (), s32[]{:S(2)}) async-start(), calls=%async_computation.8 | async-start | bytes 5308416 | tf_op jit(solution)/shard_map/reduce_scatter | solution.py:262
  428.2 11.4 %slice-start = ((s8[6291456]{0:T(1024)(128)(4,1)}), s8[4194304]{0:T(1024)(128)(4,1)S(1)}, s32[]{:S(2)}) async-start(s8[6291456]{0:T(1024)(128)(4,1)} %bitcast.224), calls=%async_computation.11 | async-start | bytes 8388608
  431.8 7.7 slice-start.1
  431.8 7.7 copy-start.21
  431.8 7.7 copy-start.23
  431.8 7.7 copy-start.24
  431.9 7.8 copy-start.93
  431.9 7.8 copy-start.94
  454.9 389.3 %all-reduce.5.cloned.1.call-start = ((), (), s32[]{:S(2)}) async-start(), calls=%async_computation.10 | async-start | bytes 36814848 | tf_op jit(solution)/shard_map/psum | solution.py:333
  502.6 4.8 copy-start.36
  502.6 4.8 copy-start.44
  502.6 4.8 copy-start.47
  502.6 4.8 copy-start.57
  502.6 4.8 copy-start.62
  502.6 4.8 copy-start.72
  502.6 8.1 copy-start.4
  510.7 6.9 copy-start.71
  528.3 5.4 copy-start.46
  528.3 5.4 copy-start.105
  531.0 5.0 copy-start.103
  531.1 7.2 copy-start.39
  541.9 42.3 %copy-start.101 = (f32[2,256]{1,0:T(2,128)S(1)}, f32[2,256]{1,0:T(2,128)}, u32[]{:S(2)}) copy-start(f32[2,256]{1,0:T(2,128)} %get-tuple-element.47) | copy-start | bytes 6148
  541.9 42.3 %copy-start.100 = (f32[2,256]{1,0:T(2,128)S(1)}, f32[2,256]{1,0:T(2,128)}, u32[]{:S(2)}) copy-start(f32[2,256]{1,0:T(2,128)} %get-tuple-element.48) | copy-start | bytes 6148
  844.2 5.6 copy-start.11
  847.0 7.8 slice-start.4
  849.7 5.0 slice-start.5
  (56 other events, 118.2 us)
Sparse Core Ops, SparseCore 0:
  9.9 41.5 all-gather.2
  53.4 38.7 all-gather.4
  371.6 52.8 reduce-scatter.4
  455.0 54.9 reduce-scatter.2
  542.0 302.0 all-reduce.4
where the time goes:
time: 875 us; the launch traced here: 867 us
  waiting for transfers between devices  415 us (47%)
  matrix products  157 us (18%)
  blocking collectives  119 us (14%)
  local copies, waits for them, and re-layouts  118 us (13%)
  other arithmetic  29 us (3%)
  between operations  15.3 us (2%)
  starting transfers between devices  14.7 us (2%)
    psum x1, waiting for transfers between devices, shards(): lax.psum((grad_qkv_weight, grad_proj, grad_ada_weight, grad_ada_bias, gra...  253 us
    all_to_all x1, blocking collectives, shards(): lax.all_to_all(dispatch_rows, 'ep', split_axis=0, concat_axis=1, tiled=True)  77.5 us
    all_to_all x1, waiting for transfers between devices, shards(): lax.all_to_all(produced, 'ep', split_axis=1, concat_axis=0, tiled=True)  65.5 us
    all_to_all x1, waiting for transfers between devices, shards(): lax.all_to_all(grad_rows, 'ep', split_axis=0, concat_axis=1, tiled=True)  60.8 us
    psum x1, blocking collectives, shards(): lax.psum((grad_qkv_weight, grad_proj, grad_ada_weight, grad_ada_bias, gra...  41.2 us
    all_to_all x1, waiting for transfers between devices, shards(): lax.all_to_all(grad_sent, 'ep', split_axis=1, concat_axis=0, tiled=True)  33.8 us
    dot_general x1, matrix products, shards(): jnp.einsum('erd,efd->erf', grad_received, back_out, preferred_element_typ...  27.1 us
    unnamed x238, local copies, waits for them, and re-layouts  26.2 us
  transfers between devices with their start and end apart: 8, of which 4 were waited for; matrix products, arithmetic and copies ran while one was open for 25% of the time, Pallas kernels for 0%

commit v1 on v0

v1 whole, which is shorter than its diff:
```python
import jax
import jax.numpy as jnp
from jax import lax
from jax.experimental import pallas as pl
from jax.experimental.pallas import tpu as pltpu
from jax.sharding import PartitionSpec as P

HEAD_DIM = 64
PATCHES = 256
ROWS = 256
GELU_SCALE = 0.7978845608028654
GELU_CUBE = 0.044715


def normalize(values):
    centred = values - jnp.mean(values, axis=-1, keepdims=True)
    inverse = lax.rsqrt(jnp.mean(centred * centred, axis=-1, keepdims=True) + 1e-06)
    return (centred * inverse, inverse)


def norm_back(grad_normed, normed, inverse):
    mean_grad = jnp.mean(grad_normed, axis=-1, keepdims=True)
    mean_cross = jnp.mean(grad_normed * normed, axis=-1, keepdims=True)
    return inverse * (grad_normed - mean_grad - normed * mean_cross)


def gelu_tanh(values):
    return jax.nn.gelu(values, approximate=True)


def gelu_back(values, grad_values):
    return jax.vjp(gelu_tanh, values)[1](grad_values)[0]


def contract(left, right, left_dim, right_dim):
    return lax.dot_general(
        left, right, (((left_dim,), (right_dim,)), ((), ())), preferred_element_type=jnp.float32
    )


def expert_kernel(
    count_ref,
    rows_ref,
    grads_ref,
    place_row_ref,
    gate_row_ref,
    place_ref,
    in_ref,
    out_ref,
    routed_ref,
    grad_rows_ref,
    grad_gate_ref,
    grad_in_ref,
    grad_out_ref,
    column_ref,
    total_in_ref,
    total_out_ref,
):
    expert, block = pl.program_id(0), pl.program_id(1)
    tokens = rows_ref.shape[0]

    @pl.when((expert == 0) & (block == 0))
    def _():
        routed_ref[...] = jnp.zeros_like(routed_ref)
        grad_rows_ref[...] = jnp.zeros_like(grad_rows_ref)

    @pl.when(block == 0)
    def _():
        lanes = lax.broadcasted_iota(jnp.int32, place_ref.shape, 1)
        column = jnp.sum(jnp.where(lanes == expert, place_ref[...], 0.0), axis=1, keepdims=True)
        column_ref[...] = jnp.broadcast_to(column, column_ref.shape)
        total_in_ref[...] = jnp.zeros_like(total_in_ref)
        total_out_ref[...] = jnp.zeros_like(total_out_ref)
        grad_gate_ref[...] = jnp.zeros_like(grad_gate_ref)

    @pl.when(block * ROWS < count_ref[expert])
    def _():
        base = (block * ROWS).astype(jnp.float32)
        row_ids = lax.broadcasted_iota(jnp.int32, (ROWS, tokens), 0).astype(jnp.float32) + base
        hit = row_ids == place_row_ref[0]
        pick = jnp.where(hit, 1.0, 0.0).astype(jnp.bfloat16)
        gate = jnp.sum(jnp.where(hit, gate_row_ref[0], 0.0), axis=1, keepdims=True)
        rows = contract(pick, rows_ref[...], 1, 0).astype(jnp.bfloat16)
        grads = contract(pick, grads_ref[...], 1, 0)
        hidden = contract(rows, in_ref[0], 1, 0)
        square = hidden * hidden
        bend = jnp.tanh(GELU_SCALE * hidden * (1.0 + GELU_CUBE * square))
        active = (0.5 * hidden * (1.0 + bend)).astype(jnp.bfloat16)
        slope = 0.5 * (1.0 + bend) + (0.5 * GELU_SCALE) * hidden * (1.0 - bend * bend) * (
            1.0 + (3.0 * GELU_CUBE) * square
        )
        produced = contract(active, out_ref[0], 1, 0).astype(jnp.bfloat16).astype(jnp.float32)
        grad_produced = (gate * grads).astype(jnp.bfloat16)
        grad_active = contract(grad_produced, out_ref[0], 1, 1)
        grad_hidden = (grad_active * slope).astype(jnp.bfloat16)
        total_in_ref[...] += contract(grad_hidden, rows, 0, 0)
        total_out_ref[...] += contract(active, grad_produced, 0, 0)
        grad_back = contract(grad_hidden, in_ref[0], 1, 1).astype(jnp.bfloat16)
        grad_gate = jnp.sum(grads * produced, axis=1, keepdims=True)
        grad_gate_ref[0] += jnp.sum(jnp.where(hit, grad_gate, 0.0), axis=0, keepdims=True)
        lane_ids = lax.broadcasted_iota(jnp.int32, (tokens, 128), 1).astype(jnp.float32) + base
        column = column_ref[...]
        place = jnp.concatenate(
            [
                jnp.where(column == lane_ids + float(start), 1.0, 0.0).astype(jnp.bfloat16)
                for start in range(0, ROWS, 128)
            ],
            axis=1,
        )
        routed_ref[...] += contract(place, (gate * produced).astype(jnp.bfloat16), 1, 0)
        grad_rows_ref[...] += contract(place, grad_back, 1, 0)

    @pl.when(block == pl.num_programs(1) - 1)
    def _():
        grad_in_ref[0] = total_in_ref[...].astype(jnp.bfloat16)
        grad_out_ref[0] = total_out_ref[...].astype(jnp.bfloat16)


def expert_stage(counts, rows, grads, place_rows, gate_rows, places, full_in, full_out):
    tokens, features = rows.shape
    experts, _, hidden = full_in.shape
    whole = lambda expert, block, counts: (0, 0)
    single = lambda expert, block, counts: (expert, 0, 0)
    row_spec = pl.BlockSpec((1, 1, tokens), single)
    weight_spec = pl.BlockSpec((1, hidden, features), single)
    token_spec = pl.BlockSpec((tokens, features), whole)
    return pl.pallas_call(
        expert_kernel,
        out_shape=(
            jax.ShapeDtypeStruct((tokens, features), jnp.float32),
            jax.ShapeDtypeStruct((tokens, features), jnp.float32),
            jax.ShapeDtypeStruct((experts, 1, tokens), jnp.float32),
            jax.ShapeDtypeStruct((experts, hidden, features), jnp.bfloat16),
            jax.ShapeDtypeStruct((experts, hidden, features), jnp.bfloat16),
        ),
        grid_spec=pltpu.PrefetchScalarGridSpec(
            num_scalar_prefetch=1,
            grid=(experts, tokens // 2 // ROWS),
            in_specs=[
                token_spec,
                token_spec,
                row_spec,
                row_spec,
                pl.BlockSpec((tokens, experts), whole),
                pl.BlockSpec((1, features, hidden), single),
                weight_spec,
            ],
            out_specs=[token_spec, token_spec, row_spec, weight_spec, weight_spec],
            scratch_shapes=[
                pltpu.VMEM((tokens, 128), jnp.float32),
                pltpu.VMEM((hidden, features), jnp.float32),
                pltpu.VMEM((hidden, features), jnp.float32),
            ],
        ),
        compiler_params=pltpu.CompilerParams(
            dimension_semantics=("arbitrary", "arbitrary"), vmem_limit_bytes=60 << 20
        ),
        name="expert_stage",
    )(counts, rows, grads, place_rows, gate_rows, places, full_in, full_out)


def place_tokens(routes, first_expert, experts):
    expert_ids = first_expert + jnp.arange(experts, dtype=jnp.int32)
    first_hit = (routes[:, 0:1] == expert_ids[None, :]).astype(jnp.float32)
    second_hit = (routes[:, 1:2] == expert_ids[None, :]).astype(jnp.float32)
    hits = first_hit + second_hit
    chunks = hits.reshape(-1, 256, experts)
    order = jnp.arange(256)
    earlier = (order[:, None] > order[None, :]).astype(jnp.bfloat16)
    within = jnp.einsum(
        "ij,cje->cie", earlier, chunks.astype(jnp.bfloat16), preferred_element_type=jnp.float32
    )
    chunk_totals = jnp.sum(chunks, axis=1)
    chunk_order = jnp.arange(chunks.shape[0])
    chunk_earlier = (chunk_order[:, None] > chunk_order[None, :]).astype(jnp.float32)
    offsets = jnp.sum(chunk_earlier[:, :, None] * chunk_totals[None, :, :], axis=1)
    places = jnp.where(chunks > 0.0, within + offsets[:, None, :], -1.0).reshape(-1, experts)
    counts = jnp.sum(chunk_totals, axis=0).astype(jnp.int32)
    return first_hit, second_hit, places, counts


def split_heads(qkv_block):
    block_count, patches, triple = qkv_block.shape
    features = triple // 3
    head_shape = (block_count, patches, features // HEAD_DIM, HEAD_DIM)
    return (
        qkv_block[..., :features].reshape(head_shape),
        qkv_block[..., features : 2 * features].reshape(head_shape),
        qkv_block[..., 2 * features :].reshape(head_shape),
    )


def attend_forward(qkv_block):
    queries, key_rows, value_rows = split_heads(qkv_block)
    score_scale = HEAD_DIM ** (-0.5)
    scores = (
        jnp.einsum("bqhd,bkhd->bhqk", queries, key_rows, preferred_element_type=jnp.float32)
        * score_scale
    )
    peak_value = jnp.max(scores, axis=-1, keepdims=True)
    shifted = jnp.exp(scores - peak_value)
    denominator = jnp.sum(shifted, axis=-1, keepdims=True)
    probability = (shifted / denominator).astype(jnp.bfloat16)
    mixed_rows = jnp.einsum(
        "bhqk,bkhd->bqhd", probability, value_rows, preferred_element_type=jnp.float32
    )
    mixed_rows = mixed_rows.reshape(qkv_block.shape[0], qkv_block.shape[1], -1).astype(jnp.bfloat16)
    return (mixed_rows, (peak_value + jnp.log(denominator))[..., 0])


def attend_backward(packed):
    qkv_block, grad_mixed, log_total = packed
    queries, key_rows, value_rows = split_heads(qkv_block)
    score_scale = HEAD_DIM ** (-0.5)
    scores = (
        jnp.einsum("bqhd,bkhd->bhqk", queries, key_rows, preferred_element_type=jnp.float32)
        * score_scale
    )
    probability = jnp.exp(scores - log_total[..., None])
    grad_heads = grad_mixed.reshape(queries.shape)
    grad_values = jnp.einsum(
        "bhqk,bqhd->bkhd",
        probability.astype(jnp.bfloat16),
        grad_heads,
        preferred_element_type=jnp.float32,
    )
    grad_probs = jnp.einsum(
        "bqhd,bkhd->bhqk", grad_heads, value_rows, preferred_element_type=jnp.float32
    )
    grad_scores = (
        probability * (grad_probs - jnp.sum(grad_probs * probability, axis=-1, keepdims=True))
    ).astype(jnp.bfloat16)
    grad_queries = (
        jnp.einsum("bhqk,bkhd->bqhd", grad_scores, key_rows, preferred_element_type=jnp.float32)
        * score_scale
    )
    grad_keys = (
        jnp.einsum("bhqk,bqhd->bkhd", grad_scores, queries, preferred_element_type=jnp.float32)
        * score_scale
    )
    merged = jnp.concatenate([grad_queries, grad_keys, grad_values], axis=2)
    return merged.reshape(qkv_block.shape[0], qkv_block.shape[1], -1).astype(jnp.bfloat16)


def shards(
    tokens,
    timesteps,
    labels,
    routes,
    time_table,
    class_table,
    ada_weight,
    ada_bias,
    gain_attn,
    gain_ffn,
    qkv_weight,
    proj_weight,
    router_weight,
    shared_in,
    shared_out,
    expert_in,
    expert_out,
    grad_out,
):
    count_tokens, features = tokens.shape
    images = count_tokens // PATCHES
    pair_count = images // 2
    ep_size = lax.axis_size("ep")
    experts = expert_in.shape[0]
    group = lax.axis_index("tg")
    device = group * ep_size + lax.axis_index("ep")
    routes_group = lax.all_gather(routes, "ep", axis=0, tiled=True)
    upstream_group = lax.all_gather(grad_out, "ep", axis=0, tiled=True)
    full_in = lax.all_gather(expert_in, "tg", axis=2, tiled=True)
    full_out = lax.all_gather(expert_out, "tg", axis=1, tiled=True)
    step_ids = jnp.arange(time_table.shape[0], dtype=jnp.int32)
    class_ids = jnp.arange(class_table.shape[0], dtype=jnp.int32)
    time_hot = (timesteps[:, None] == step_ids[None, :]).astype(jnp.bfloat16)
    class_hot = (labels[:, None] == class_ids[None, :]).astype(jnp.bfloat16)
    condition = jnp.dot(time_hot, time_table, preferred_element_type=jnp.float32) + jnp.dot(
        class_hot, class_table, preferred_element_type=jnp.float32
    )
    silu_low = jax.nn.silu(condition).astype(jnp.bfloat16)
    all_modulation = jnp.dot(silu_low, ada_weight, preferred_element_type=jnp.float32) + ada_bias
    modulation = lax.dynamic_slice_in_dim(all_modulation, device * images, images).reshape(
        images, 6, 1, features
    )
    group_gate = lax.dynamic_slice_in_dim(
        all_modulation[:, 5 * features :], group * images * ep_size, images * ep_size
    )
    grad_group = (
        (group_gate[:, None, :] * upstream_group.reshape(-1, PATCHES, features))
        .astype(jnp.bfloat16)
        .reshape(-1, features)
    )
    first_hit, second_hit, places, counts = place_tokens(
        routes_group, lax.axis_index("ep") * experts, experts
    )
    residual = tokens.astype(jnp.float32).reshape(images, PATCHES, features)
    normed_attn, inverse_attn = normalize(residual)
    factor_attn = 1.0 + modulation[:, 1]
    attn_in = (
        (normed_attn * gain_attn * factor_attn + modulation[:, 0])
        .astype(jnp.bfloat16)
        .reshape(-1, features)
    )
    qkv_rows = jnp.dot(attn_in, qkv_weight, preferred_element_type=jnp.float32).astype(jnp.bfloat16)
    qkv_blocks = qkv_rows.reshape(pair_count, 2, PATCHES, 3 * features)
    mixed_rows, log_total = lax.map(attend_forward, qkv_blocks)
    mixed_rows = mixed_rows.reshape(-1, features)
    attn_out = jnp.dot(mixed_rows, proj_weight, preferred_element_type=jnp.float32).reshape(
        images, PATCHES, features
    )
    middle = residual + modulation[:, 2] * attn_out
    normed_ffn, inverse_ffn = normalize(middle)
    factor_ffn = 1.0 + modulation[:, 4]
    ffn_in = (
        (normed_ffn * gain_ffn * factor_ffn + modulation[:, 3])
        .astype(jnp.bfloat16)
        .reshape(-1, features)
    )
    rows_group = lax.all_gather(ffn_in, "ep", axis=0, tiled=True)
    shared_hidden = jnp.dot(ffn_in, shared_in, preferred_element_type=jnp.float32)
    shared_active = gelu_tanh(shared_hidden).astype(jnp.bfloat16)
    shared_term = jnp.dot(shared_active, shared_out, preferred_element_type=jnp.float32)
    upstream = grad_out.astype(jnp.float32).reshape(images, PATCHES, features)
    grad_ffn = (modulation[:, 5] * upstream).reshape(-1, features)
    grad_shared_low = grad_ffn.astype(jnp.bfloat16)
    grad_shared_out = jnp.einsum(
        "rf,rd->fd", shared_active, grad_shared_low, preferred_element_type=jnp.float32
    )
    grad_shared_active = jnp.einsum(
        "rd,fd->rf", grad_shared_low, shared_out, preferred_element_type=jnp.float32
    )
    grad_shared_hidden = gelu_back(shared_hidden, grad_shared_active).astype(jnp.bfloat16)
    grad_shared_in = jnp.einsum(
        "rd,rf->df", ffn_in, grad_shared_hidden, preferred_element_type=jnp.float32
    )
    grad_ffn_in = jnp.einsum(
        "rf,df->rd", grad_shared_hidden, shared_in, preferred_element_type=jnp.float32
    )
    route_ids = jnp.arange(router_weight.shape[1], dtype=jnp.int32)
    first_hot = (routes_group[:, 0:1] == route_ids[None, :]).astype(jnp.float32)
    second_hot = (routes_group[:, 1:2] == route_ids[None, :]).astype(jnp.float32)
    logits = jnp.dot(rows_group, router_weight, preferred_element_type=jnp.float32)
    first_logit = jnp.sum(logits * first_hot, axis=1, keepdims=True)
    second_logit = jnp.sum(logits * second_hot, axis=1, keepdims=True)
    peak_logit = jnp.maximum(first_logit, second_logit)
    first_power = jnp.exp(first_logit - peak_logit)
    second_power = jnp.exp(second_logit - peak_logit)
    first_gate = first_power / (first_power + second_power)
    second_gate = second_power / (first_power + second_power)
    gates_here = first_hit * first_gate + second_hit * second_gate
    routed_part, grad_rows_part, grad_gates, grad_in_part, grad_out_part = expert_stage(
        counts,
        rows_group,
        grad_group,
        places.T[:, None, :],
        gates_here.T[:, None, :],
        places,
        full_in,
        full_out,
    )
    grad_hits = grad_gates[:, 0, :].T
    gate_pull = (
        first_gate
        * second_gate
        * jnp.sum(grad_hits * (first_hit - second_hit), axis=1, keepdims=True)
    )
    grad_logits = gate_pull * (first_hot - second_hot)
    grad_router = jnp.einsum(
        "rd,re->de",
        rows_group.astype(jnp.float32),
        grad_logits,
        precision=lax.Precision.HIGHEST,
    )
    grad_rows_part = grad_rows_part + jnp.einsum(
        "re,de->rd", grad_logits, router_weight.astype(jnp.float32), precision=lax.Precision.HIGHEST
    )
    grad_ffn_in = grad_ffn_in + lax.psum_scatter(
        grad_rows_part.astype(jnp.bfloat16), "ep", scatter_dimension=0, tiled=True
    ).astype(jnp.float32)
    routed = lax.psum_scatter(
        routed_part.astype(jnp.bfloat16), "ep", scatter_dimension=0, tiled=True
    ).astype(jnp.float32)
    ffn_out = (routed + shared_term).reshape(images, PATCHES, features)
    output = (middle + modulation[:, 5] * ffn_out).reshape(-1, features).astype(jnp.bfloat16)
    grad_gate_ffn = jnp.sum(upstream * ffn_out, axis=1)
    shard_in = (
        lax.psum_scatter(grad_in_part, "tg", scatter_dimension=1, tiled=True)
        .astype(jnp.float32)
        .transpose(0, 2, 1)
    )
    shard_out = lax.psum_scatter(grad_out_part, "tg", scatter_dimension=1, tiled=True).astype(
        jnp.float32
    )
    grad_ffn_cube = grad_ffn_in.reshape(images, PATCHES, features)
    grad_shift_ffn = jnp.sum(grad_ffn_cube, axis=1)
    cross_ffn = jnp.sum(grad_ffn_cube * normed_ffn, axis=1)
    grad_middle = upstream + norm_back(
        grad_ffn_cube * gain_ffn * factor_ffn, normed_ffn, inverse_ffn
    )
    grad_gate_attn = jnp.sum(grad_middle * attn_out, axis=1)
    grad_attn_low = (modulation[:, 2] * grad_middle).reshape(-1, features).astype(jnp.bfloat16)
    grad_proj = jnp.einsum(
        "rd,re->de", mixed_rows, grad_attn_low, preferred_element_type=jnp.float32
    )
    grad_mixed = jnp.einsum(
        "re,de->rd", grad_attn_low, proj_weight, preferred_element_type=jnp.float32
    ).astype(jnp.bfloat16)
    grad_qkv = lax.map(
        attend_backward,
        (qkv_blocks, grad_mixed.reshape(pair_count, 2, PATCHES, features), log_total),
    ).reshape(-1, 3 * features)
    grad_qkv_weight = jnp.einsum("rd,re->de", attn_in, grad_qkv, preferred_element_type=jnp.float32)
    grad_attn_in = jnp.einsum(
        "re,de->rd", grad_qkv, qkv_weight, preferred_element_type=jnp.float32
    ).reshape(images, PATCHES, features)
    grad_shift_attn = jnp.sum(grad_attn_in, axis=1)
    cross_attn = jnp.sum(grad_attn_in * normed_attn, axis=1)
    grad_tokens = grad_middle + norm_back(
        grad_attn_in * gain_attn * factor_attn, normed_attn, inverse_attn
    )
    image_sums = lax.all_gather(
        jnp.concatenate(
            [
                grad_shift_attn,
                cross_attn,
                grad_gate_attn,
                grad_shift_ffn,
                cross_ffn,
                grad_gate_ffn,
            ],
            axis=1,
        ),
        ("tg", "ep"),
        axis=0,
        tiled=True,
    ).reshape(-1, 6, features)
    all_pieces = all_modulation.reshape(-1, 6, features)
    grad_gain_attn = jnp.sum(image_sums[:, 1] * (1.0 + all_pieces[:, 1]), axis=0)
    grad_gain_ffn = jnp.sum(image_sums[:, 4] * (1.0 + all_pieces[:, 4]), axis=0)
    ones = jnp.ones_like(gain_attn)
    piece_gains = jnp.stack([ones, gain_attn, ones, ones, gain_ffn, ones])
    grad_modulation = (image_sums * piece_gains).reshape(-1, 6 * features)
    grad_ada_bias = jnp.sum(grad_modulation, axis=0)
    grad_ada_weight = jnp.einsum(
        "id,ie->de", silu_low.astype(jnp.float32), grad_modulation, precision=lax.Precision.HIGHEST
    )
    grad_silu = jnp.einsum(
        "ie,de->id",
        grad_modulation,
        ada_weight.astype(jnp.float32),
        precision=lax.Precision.HIGHEST,
    )
    grad_condition = jax.vjp(jax.nn.silu, condition)[1](grad_silu)[0]
    time_term = jnp.einsum(
        "is,id->sd", time_hot.astype(jnp.float32), grad_condition, precision=lax.Precision.HIGHEST
    )
    class_term = jnp.einsum(
        "ic,id->cd", class_hot.astype(jnp.float32), grad_condition, precision=lax.Precision.HIGHEST
    )
    low_sums = lax.psum(
        tuple(
            item.astype(jnp.bfloat16)
            for item in (grad_shared_in, grad_shared_out, grad_qkv_weight, grad_proj, grad_router)
        ),
        ("tg", "ep"),
    )
    shared_in_sum, shared_out_sum, qkv_sum, proj_sum, router_sum = (
        item.astype(jnp.float32) for item in low_sums
    )
    return (
        output,
        grad_tokens.reshape(-1, features),
        time_term,
        class_term,
        grad_ada_weight,
        grad_ada_bias,
        grad_gain_attn,
        grad_gain_ffn,
        qkv_sum,
        proj_sum,
        router_sum,
        shared_in_sum,
        shared_out_sum,
        shard_in,
        shard_out,
    )


def solution(mesh):
    in_specs = (
        P(("tg", "ep"), None),
        P(),
        P(),
        P(("tg", "ep"), None),
        P(),
        P(),
        P(),
        P(),
        P(),
        P(),
        P(),
        P(),
        P(),
        P(),
        P(),
        P("ep", None, "tg"),
        P("ep", "tg", None),
        P(("tg", "ep"), None),
    )
    out_specs = (
        P(("tg", "ep"), None),
        P(("tg", "ep"), None),
        P(),
        P(),
        P(),
        P(),
        P(),
        P(),
        P(),
        P(),
        P(),
        P(),
        P(),
        P("ep", None, "tg"),
        P("ep", "tg", None),
    )
    return jax.shard_map(shards, mesh=mesh, in_specs=in_specs, out_specs=out_specs, check_vma=False)
```

time: 875 us -> 611 us (0.70)
  waiting for transfers between devices: 415 us -> 245 us
  matrix products: 157 us -> 75.4 us
  local copies, waits for them, and re-layouts: 118 us -> 42 us
  Pallas kernels: 0 us -> 55.3 us
  starting transfers between devices: 14.7 us -> 0.36 us
  blocking collectives: 119 us -> 133 us
  other arithmetic: 29 us -> 40.6 us
    psum x1, waiting for transfers between devices: 253 us -> 6.97 us  [shards(): lax.psum(tuple((item.astype(jnp.bfloat16) for item in (grad_shared_in, gr...]
    all_to_all x3 -> x0, waiting for transfers between devices: 160 us -> none  [the longest x1 65.5 us: shards(): lax.all_to_all(produced, 'ep', split_axis=1, concat_axis=0, tiled=True)]
    reduce_scatter x2 -> x4, waiting for transfers between devices: 0.01 us -> 139 us  [the longest x1 55.1 us: shards(): lax.psum_scatter(grad_out_part, 'tg', scatter_dimension=1, tiled=True)]
    all_gather x2 -> x4, waiting for transfers between devices: 0.01 us -> 96.1 us  [the longest x1 36.2 us: shards(): full_in = lax.all_gather(expert_in, 'tg', axis=2, tiled=True)]
    all_gather x0 -> x2, blocking collectives: none -> 93.3 us  [the longest x1 77.7 us: shards(): lax.all_gather(jnp.concatenate([grad_shift_attn, cross_attn, grad_gate_at...]
    dot_general x8 -> x3, matrix products: 92.1 us -> 5.67 us  [the longest x1 2.14 us: shards(): jnp.einsum('rd,re->de', rows_group.astype(jnp.float32), grad_logits, prec...]
    all_to_all x1 -> x0, blocking collectives: 77.5 us -> none  [shards(): lax.all_to_all(dispatch_rows, 'ep', split_axis=0, concat_axis=1, tiled=True)]
    pallas_call x0 -> x1, Pallas kernels: none -> 55.3 us  [expert_stage(): pl.pallas_call(expert_kernel, out_shape=(jax.ShapeDtypeStruct((tokens, fe...]
  transfers between devices with their start and end apart: 8 -> 9, of which waited for: 4 -> 8; matrix products, arithmetic and copies ran while one was open for 25% -> 21% of each run, Pallas kernels for 0% -> 0%
where the time goes in v1:
time: 611 us; the launch traced here: 607 us
  waiting for transfers between devices  245 us (40%)
  blocking collectives  133 us (22%)
  matrix products  75.4 us (12%)
  Pallas kernels  55.3 us (9%)
  local copies, waits for them, and re-layouts  42 us (7%)
  other arithmetic  40.6 us (7%)
  between operations  15.1 us (2%)
    all_gather x1, blocking collectives, shards(): lax.all_gather(jnp.concatenate([grad_shift_attn, cross_attn, grad_gate_at...  77.7 us
    pallas_call x1, Pallas kernels, expert_stage(): pl.pallas_call(expert_kernel, out_shape=(jax.ShapeDtypeStruct((tokens, fe...  55.3 us
    reduce_scatter x1, waiting for transfers between devices, shards(): lax.psum_scatter(grad_out_part, 'tg', scatter_dimension=1, tiled=True)  55.1 us
    reduce_scatter x1, waiting for transfers between devices, shards(): lax.psum_scatter(grad_in_part, 'tg', scatter_dimension=1, tiled=True)  46.7 us
    psum x1, blocking collectives, shards(): lax.psum(tuple((item.astype(jnp.bfloat16) for item in (grad_shared_in, gr...  40.1 us
    all_gather x1, waiting for transfers between devices, shards(): full_in = lax.all_gather(expert_in, 'tg', axis=2, tiled=True)  36.2 us
    all_gather x1, waiting for transfers between devices, shards(): full_out = lax.all_gather(expert_out, 'tg', axis=1, tiled=True)  32.2 us
    all_gather x1, waiting for transfers between devices, shards(): rows_group = lax.all_gather(ffn_in, 'ep', axis=0, tiled=True)  27.7 us
  transfers between devices with their start and end apart: 9, of which 8 were waited for; matrix products, arithmetic and copies ran while one was open for 21% of the time, Pallas kernels for 0%

profile of v1, /device:TPU:0, one launch (start us, length us, event | category | flops | bytes accessed | tf_op | source)
XLA Modules:
  0.0 606.9 jit_solution(1176531033954635652)
XLA Ops:
  8.0 1.5 fusion.44
  9.5 1.5 convolution_add_fusion.3
  11.0 1.9 convolution_add_fusion
  17.7 1.3 copy.89
  22.1 1.3 multiply_add_fusion.2
  24.9 2.3 copy.93
  27.9 1.5 slice.88
  29.5 15.6 %all_gather.18 = s32[2048,2]{0,1:T(2,128)S(1)} all-gather(s32[512,2]{0,1:T(2,128)} %param.21), channel_id=1, replica_groups=mesh['tg'=8,'ep'=4] {'ep'}, dimensions={0}, use_global_device_ids=true | all-gather | bytes 20480 | tf_op jit(solution)/shard_map/all_gather | solution.py:272
  45.8 1.3 eq.132
  47.1 1.3 eq.128
  49.9 1.6 fusion.23
  51.5 2.1 copy.92
  53.6 2.2 copy.94.place_row_ref
  55.7 1.3 constant_dynamic-slice_fusion
  57.0 3.0 fusion.7.grads_ref
  60.0 27.7 %all-gather.6.cloned.1.call-done.rows_ref = bf16[2048,384]{1,0:T(8,128)(2,1)} async-done(((bf16[512,384]{1,0:T(8,128)(2,1)}), bf16[2048,384]{1,0:T(8,128)(2,1)}) %all-gather.6.cloned.1.call-update) | async-done | bytes 1572880 | tf_op jit(solution)/shard_map/all_gather | solution.py:322
  87.7 1.9 select_reduce_fusion.1
  90.3 1.3 fusion.65.gate_row_ref
  91.6 36.2 %all-gather.10.cloned.1.call-done = bf16[4,384,1536]{1,0,2:T(4,128)(2,1)} async-done(((bf16[4,384,192]{1,0,2:T(4,128)(2,1)}), bf16[4,384,1536]{1,0,2:T(4,128)(2,1)}) %all-gather.10.cloned.1.call-update) | async-done | bytes 4718608 | tf_op jit(solution)/shard_map/all_gather | solution.py:274
  127.8 8.4 %copy.95.in_ref = bf16[4,384,1536]{2,1,0:T(8,128)(2,1)} copy(bf16[4,384,1536]{1,0,2:T(4,128)(2,1)} %all-gather.10.cloned.1.call-done) | data formatting | bytes 9437184 | tf_op jit(solution)/shard_map/all_gather | solution.py:274
  136.2 32.2 %all-gather.12.cloned.1.call-done.out_ref = bf16[4,1536,384]{2,1,0:T(8,128)(2,1)} async-done(((bf16[4,192,384]{2,1,0:T(8,128)(2,1)}), bf16[4,1536,384]{2,1,0:T(8,128)(2,1)}) %all-gather.12.cloned.1.call-update) | async-done | bytes 4718608 | tf_op jit(solution)/shard_map/all_gather | solution.py:275
  168.4 55.3 %expert_stage.1 = (f32[2048,384]{1,0:T(8,128)}, f32[2048,384]{1,0:T(8,128)}, f32[4,1,2048]{2,1,0:T(1,128)}, bf16[4,1536,384]{2,1,0:T(8,128)(2,1)}, bf16[4,1536,384]{2,1,0:T(8,128)(2,1)}) custom-call(s32[4]{0:T(128)} %convert_element_type.195.count_ref, bf16[2048,384]{1,0:T(8,128)(2,1)} %all-gather.6.cloned.1.call-done.rows_ref, ...), custom_call_target="tpu_custom_call" | custom-call | tf_op jit(solution)/shard_map/expert_stage/pallas_call | solution.py:127
  225.3 4.5 add_convert_fusion
  229.9 2.0 fusion.27
  231.9 1.4 copy.105
  234.1 1.3 log_add_fusion
  235.4 5.6 fusion.83
  241.0 1.4 convert_element_type.201
  242.5 7.6 %fusion.6 = bf16[512,3072]{1,0:T(8,128)(2,1)S(1)} fusion(f32[512,3072]{1,0:T(8,128)} %fusion.83, bf16[512,384]{1,0:T(8,128)(2,1)} %fusion.27, bf16[3072,384]{1,0:T(8,128)(2,1)S(1)} %copy-done), kind=kOutput, calls=%fused_computation.8 | convolution fusion | flops 1239416832 | bytes 12189696 | tf_op jit(solution)/shard_map/rd,fd->rf/dot_general | solution.py:332
  250.1 1.7 copy-done.3
  251.8 2.8 convolution_convert_fusion.1
  254.6 7.0 %convolution_convert_fusion = bf16[3072,384]{1,0:T(8,128)(2,1)} fusion(bf16[512,384]{1,0:T(8,128)(2,1)S(1)} %copy-done.33, f32[512,3072]{1,0:T(8,128)} %fusion.83), kind=kOutput, calls=%fused_computation.10 | convolution fusion | flops 1223294976 | bytes 9043968 | tf_op jit(solution)/shard_map/rf,rd->fd/dot_general | solution.py:329
  261.6 11.1 %reduce-scatter.7.cloned.1.call-done = bf16[512,384]{1,0:T(8,128)(2,1)} async-done(((bf16[2048,384]{1,0:T(8,128)(2,1)}), bf16[512,384]{1,0:T(8,128)(2,1)}) %reduce-scatter.7.cloned.1.call-update) | async-done | bytes 393232 | tf_op jit(solution)/shard_map/reduce_scatter | solution.py:380
  272.7 5.4 fusion.26
  278.7 1.3 div.78
  280.0 2.5 fusion.28
  283.1 26.1 %reduce-scatter.5.cloned.1.call-done = bf16[512,384]{1,0:T(8,128)(2,1)} async-done(((bf16[2048,384]{1,0:T(8,128)(2,1)}), bf16[512,384]{1,0:T(8,128)(2,1)}) %reduce-scatter.5.cloned.1.call-update) | async-done | bytes 393232 | tf_op jit(solution)/shard_map/reduce_scatter | solution.py:383
  309.3 5.9 multiply_reduce_fusion.2
  315.3 1.8 multiply_reduce_fusion.3
  319.4 1.1 reshape.486
  320.5 2.7 fusion.16
  326.5 1.1 convolution_convert_fusion.4
  328.7 1.6 fusion.8
  333.3 2.1 convolution_convert_fusion.5
  335.5 40.1 %psum.37 = bf16[384,16]{0,1:T(8,128)(2,1)S(1)} all-reduce(bf16[384,16]{0,1:T(8,128)(2,1)S(1)} %convolution_convert_fusion.5), channel_id=1, replica_groups=mesh['tg'=8,'ep'=4] {'tg','ep'}, use_global_device_ids=true, to_apply=%region_30.31 | all-reduce | flops 6144 | bytes 24576 | tf_op jit(solution)/shard_map/psum | solution.py:463
  376.2 3.5 fusion.30
  379.8 77.7 %all-gather = f32[32,2,2304]{2,1,0:T(2,128)} all-gather(f32[1,2,2304]{2,1,0:T(2,128)S(1)} %bitcast.188), channel_id=1, replica_groups=mesh['tg'=8,'ep'=4] {'tg','ep'}, dimensions={0}, use_global_device_ids=true | all-gather | bytes 608256 | tf_op jit(solution)/shard_map/all_gather | solution.py:424
  457.5 1.5 reshape.491
  459.0 2.4 reshape.488
  462.1 3.0 fusion.58
  465.1 3.2 fusion.52
  468.4 2.2 fusion.43
  470.6 2.2 fusion.42
  472.8 1.2 multiply_add_fusion
  474.1 3.4 fusion.31
  477.5 7.0 %all-reduce.3.cloned.1.call-done = (bf16[384,1152]{1,0:T(8,128)(2,1)}, bf16[384,384]{1,0:T(8,128)(2,1)}, bf16[384,3072]{1,0:T(8,128)(2,1)}, bf16[3072,384]{1,0:T(8,128)(2,1)}) async-done(((bf16[384,1152]{1,0:T(8,128)(2,1)}, bf16[384,384]{1,0:T(8,128)(2,1)}, bf16[384,3072]{1,0:T(8,128)(2,1)}, bf16[3072,384]{1,0:T(8,128)(2,1)}), (bf16[384,1152]{1,0:T(8,128)(2,1)}, bf16[384,384]{1,0:T(8,128)(2,1)}, ...) | async-done | bytes 5898256 | tf_op jit(solution)/shard_map/psum | solution.py:463
  484.4 2.6 convert_element_type.224
  487.1 1.8 convert_element_type.227
  488.9 2.8 convert_element_type.231
  491.7 2.5 convert_element_type.233
  494.1 46.7 %reduce-scatter.9.cloned.1.call-done = bf16[4,192,384]{2,1,0:T(8,128)(2,1)} async-done(((bf16[4,1536,384]{2,1,0:T(8,128)(2,1)}), bf16[4,192,384]{2,1,0:T(8,128)(2,1)}) %reduce-scatter.9.cloned.1.call-update) | async-done | bytes 589840 | tf_op jit(solution)/shard_map/reduce_scatter | solution.py:390
  540.8 2.2 convert_bitcast_fusion
  543.0 55.1 %reduce-scatter.11.cloned.1.call-done = bf16[4,192,384]{2,1,0:T(8,128)(2,1)} async-done(((bf16[4,1536,384]{2,1,0:T(8,128)(2,1)}), bf16[4,192,384]{2,1,0:T(8,128)(2,1)}) %reduce-scatter.11.cloned.1.call-update) | async-done | bytes 589840 | tf_op jit(solution)/shard_map/reduce_scatter | solution.py:394
  598.1 2.2 convert_element_type.234
  (239 shorter events, 27.7 us)
Async XLA Ops:
  7.2 235.3 %copy-start = (bf16[3072,384]{1,0:T(8,128)(2,1)S(1)}, bf16[3072,384]{1,0:T(8,128)(2,1)}, u32[]{:S(2)}) copy-start(bf16[3072,384]{1,0:T(8,128)(2,1)} %param.32) | copy-start | bytes 7077892
  7.2 6.4 %copy-start.5 = (bf16[512,384]{1,0:T(8,128)(2,1)S(1)}, bf16[512,384]{1,0:T(8,128)(2,1)}, u32[]{:S(2)}) copy-start(bf16[512,384]{1,0:T(8,128)(2,1)} %param.18) | copy-start | bytes 1179652
  7.2 7.4 %copy-start.63 = (f32[384]{0:T(512)S(1)}, f32[384]{0:T(512)}, u32[]{:S(2)}) copy-start(f32[384]{0:T(512)} %param.26) | copy-start | bytes 4612
  7.2 49.8 %all-gather.8.cloned.1.call-start = ((), (), s32[]{:S(2)}) async-start(), calls=%async_computation.5 | async-start | bytes 1966080 | tf_op jit(solution)/shard_map/all_gather | solution.py:273
  8.0 79.7 %all-gather.6.cloned.1.call-start = ((), (), s32[]{:S(2)}) async-start(), calls=%async_computation.4 | async-start | bytes 1966080 | tf_op jit(solution)/shard_map/all_gather | solution.py:322
  9.5 5.4 copy-start.31
  11.0 3.1 copy-start.20
  13.6 7.7 %copy-start.60 = (f32[2,384]{1,0:T(2,128)}, f32[2,384]{1,0:T(2,128)S(1)}, u32[]{:S(2)}) copy-start(f32[2,384]{1,0:T(2,128)S(1)} %get-tuple-element.84) | copy-start | bytes 9220
  13.6 10.2 %copy-start.38 = (f32[2,384]{1,0:T(2,128)}, f32[2,384]{1,0:T(2,128)S(1)}, u32[]{:S(2)}) copy-start(f32[2,384]{1,0:T(2,128)S(1)} %get-tuple-element.81) | copy-start | bytes 9220
  14.9 1.7 copy-start.22
  17.7 2.6 copy-start.10
  20.3 1.8 copy-start.29
  21.3 2.5 copy-start.47
  24.9 103.0 %all-gather.10.cloned.1.call-start = ((), (), s32[]{:S(2)}) async-start(), calls=%async_computation.6 | async-start | bytes 5308416 | tf_op jit(solution)/shard_map/all_gather | solution.py:274
  27.3 141.1 %all-gather.12.cloned.1.call-start = ((), (), s32[]{:S(2)}) async-start(), calls=%async_computation.7 | async-start | bytes 5308416 | tf_op jit(solution)/shard_map/all_gather | solution.py:275
  27.9 244.9 %reduce-scatter.7.cloned.1.call-start = ((), (), s32[]{:S(2)}) async-start(), calls=%async_computation.9 | async-start | bytes 1966080 | tf_op jit(solution)/shard_map/reduce_scatter | solution.py:380
  168.4 55.3 %copy-start.78 = (s32[4]{0:T(128)S(1)}, s32[4]{0:T(128)}, u32[]{:S(2)}) copy-start(s32[4]{0:T(128)} %copy-done.77) | copy-start | bytes 52
  168.4 56.2 %copy-start.43 = (f32[2048]{0:T(1024)S(1)}, f32[2048]{0:T(1024)}, u32[]{:S(2)}) copy-start(f32[2048]{0:T(1024)} %copy-done.42) | copy-start | bytes 24580
  168.4 56.2 %copy-start.45 = (f32[2048]{0:T(1024)S(1)}, f32[2048]{0:T(1024)}, u32[]{:S(2)}) copy-start(f32[2048]{0:T(1024)} %copy-done.44) | copy-start | bytes 24580
  168.4 56.8 %copy-start.52 = (bf16[384,16]{0,1:T(8,128)(2,1)S(1)}, bf16[384,16]{0,1:T(8,128)(2,1)}, u32[]{:S(2)}) copy-start(bf16[384,16]{0,1:T(8,128)(2,1)} %param.30) | copy-start | bytes 36868
  229.8 79.4 %reduce-scatter.5.cloned.1.call-start = ((), (), s32[]{:S(2)}) async-start(), calls=%async_computation.8 | async-start | bytes 1966080 | tf_op jit(solution)/shard_map/reduce_scatter | solution.py:383
  229.9 5.5 copy-start.6
  235.4 5.6 copy-start.14
  242.4 242.0 %all-reduce.3.cloned.1.call-start = ((), (), s32[]{:S(2)}) async-start(), calls=%async_computation.12 | async-start | bytes 11796480 | tf_op jit(solution)/shard_map/psum | solution.py:463
  242.5 9.3 %copy-start.9 = (bf16[2,256,384]{2,1,0:T(8,128)(2,1)S(1)}, bf16[2,256,384]{2,1,0:T(8,128)(2,1)}, u32[]{:S(2)}) copy-start(bf16[2,256,384]{2,1,0:T(8,128)(2,1)} %add_convert_fusion.2) | copy-start | bytes 1179652
  251.7 2.8 copy-start.33
  309.2 6.0 copy-start.4
  309.2 6.0 copy-start.15
  309.2 6.0 copy-start.39
  309.2 6.0 copy-start.48
  309.2 6.0 copy-start.51
  309.2 6.0 copy-start.56
  309.2 6.0 copy-start.62
  309.3 6.0 copy-start.75
  309.3 6.0 copy-start.76
  315.2 2.7 copy-start.61
  315.3 2.7 copy-start.30
  320.5 2.9 copy-start.2
  320.5 2.9 copy-start.25
  320.5 2.9 copy-start.34
  325.9 2.8 copy-start.23
  330.4 210.4 %reduce-scatter.9.cloned.1.call-start = ((), (), s32[]{:S(2)}) async-start(), calls=%async_computation.10 | async-start | bytes 5308416 | tf_op jit(solution)/shard_map/reduce_scatter | solution.py:390
  331.2 2.1 copy-start.41
  331.2 266.9 %reduce-scatter.11.cloned.1.call-start = ((), (), s32[]{:S(2)}) async-start(), calls=%async_computation.11 | async-start | bytes 5308416 | tf_op jit(solution)/shard_map/reduce_scatter | solution.py:394
  331.2 45.0 %copy-start.58 = (f32[2,384]{1,0:T(2,128)S(1)}, f32[2,384]{1,0:T(2,128)}, u32[]{:S(2)}) copy-start(f32[2,384]{1,0:T(2,128)} %copy-done.57) | copy-start | bytes 9220
  332.0 47.8 %copy-start.71 = (f32[2,256]{1,0:T(2,128)}, f32[2,256]{1,0:T(2,128)S(1)}, u32[]{:S(2)}) copy-start(f32[2,256]{1,0:T(2,128)S(1)} %rsqrt.22) | copy-start | bytes 6148
  332.0 47.7 %copy-start.73 = (f32[2,256]{1,0:T(2,128)}, f32[2,256]{1,0:T(2,128)S(1)}, u32[]{:S(2)}) copy-start(f32[2,256]{1,0:T(2,128)S(1)} %div.81) | copy-start | bytes 6148
  333.3 128.2 %copy-start.35 = (f32[2304]{0:T(1024)}, f32[2304]{0:T(1024)S(1)}, u32[]{:S(2)}) copy-start(f32[2304]{0:T(1024)S(1)} %mul.475) | copy-start | bytes 27652
  335.4 44.3 %copy-start.70 = (f32[2,384]{1,0:T(2,128)S(1)}, f32[2,384]{1,0:T(2,128)}, u32[]{:S(2)}) copy-start(f32[2,384]{1,0:T(2,128)} %get-tuple-element.73) | copy-start | bytes 9220
  335.4 44.4 %copy-start.69 = (f32[2,384]{1,0:T(2,128)S(1)}, f32[2,384]{1,0:T(2,128)}, u32[]{:S(2)}) copy-start(f32[2,384]{1,0:T(2,128)} %get-tuple-element.59) | copy-start | bytes 9220
  335.4 44.4 %copy-start.68 = (f32[2,384]{1,0:T(2,128)S(1)}, f32[2,384]{1,0:T(2,128)}, u32[]{:S(2)}) copy-start(f32[2,384]{1,0:T(2,128)} %get-tuple-element.57) | copy-start | bytes 9220
  335.4 44.4 %copy-start.79 = (f32[2,384]{1,0:T(2,128)S(1)}, f32[2,384]{1,0:T(2,128)}, u32[]{:S(2)}) copy-start(f32[2,384]{1,0:T(2,128)} %get-tuple-element.71) | copy-start | bytes 9220
  379.7 85.4 %copy-start.21 = (f32[64,384]{1,0:T(8,128)S(1)}, f32[64,384]{1,0:T(8,128)}, u32[]{:S(2)}) copy-start(f32[64,384]{1,0:T(8,128)} %copy-done.20) | copy-start | bytes 294916
  457.5 10.9 %copy-start.81 = (s32[64]{0:T(128)S(1)}, s32[64]{0:T(128)}, u32[]{:S(2)}) copy-start(s32[64]{0:T(128)} %param.19) | copy-start | bytes 772
  459.0 11.6 %copy-start.80 = (s32[64]{0:T(128)S(1)}, s32[64]{0:T(128)}, u32[]{:S(2)}) copy-start(s32[64]{0:T(128)} %param.20) | copy-start | bytes 772
  462.1 10.7 %copy-start.8 = (f32[2,256,384]{2,1,0:T(8,128)S(1)}, f32[2,256,384]{2,1,0:T(8,128)}, u32[]{:S(2)}) copy-start(f32[2,256,384]{2,1,0:T(8,128)} %copy-done.7) | copy-start | bytes 2359300
  462.1 10.7 %copy-start.32 = (f32[2,256,384]{2,1,0:T(8,128)S(1)}, f32[2,256,384]{2,1,0:T(8,128)}, u32[]{:S(2)}) copy-start(f32[2,256,384]{2,1,0:T(8,128)} %get-tuple-element.98) | copy-start | bytes 2359300
  462.1 10.7 %copy-start.59 = (f32[2,384]{1,0:T(2,128)S(1)}, f32[2,384]{1,0:T(2,128)}, u32[]{:S(2)}) copy-start(f32[2,384]{1,0:T(2,128)} %copy-done.57) | copy-start | bytes 9220
  462.1 10.7 %copy-start.65 = (f32[384]{0:T(512)S(1)}, f32[384]{0:T(512)}, u32[]{:S(2)}) copy-start(f32[384]{0:T(512)} %param.26) | copy-start | bytes 4612
  462.1 10.7 %copy-start.72 = (f32[2,256]{1,0:T(2,128)S(1)}, f32[2,256]{1,0:T(2,128)}, u32[]{:S(2)}) copy-start(f32[2,256]{1,0:T(2,128)} %copy-done.71) | copy-start | bytes 6148
  462.1 10.7 %copy-start.74 = (f32[2,256]{1,0:T(2,128)S(1)}, f32[2,256]{1,0:T(2,128)}, u32[]{:S(2)}) copy-start(f32[2,256]{1,0:T(2,128)} %copy-done.73) | copy-start | bytes 6148
  468.4 5.7 copy-start.36
  484.4 4.5 copy-start.19
  488.9 2.8 copy-start.18
  (27 other events, 27.8 us)
Sparse Core Ops, SparseCore 0:
  9.6 40.0 all-gather.7
  51.8 35.8 all-gather.5
  90.2 37.6 all-gather.9
  129.6 38.7 all-gather.11
  229.9 42.7 reduce-scatter.6
  274.9 34.2 reduce-scatter.4
  330.5 153.8 all-reduce.2
  487.9 52.8 reduce-scatter.8
  544.3 53.7 reduce-scatter.10
